TPU v7x, 32 devices: a whole 2x2x4 slice. The times are simulated.
32 devices in a mesh: row: 4 (over y, x), col: 8 (over z, core).
Axes of the slice: x: 2, y: 2, z: 4, core: 2. Of those that a mesh axis runs over, the one named last changes fastest.
Arguments:
- parent_entries: float32 [16384, 16384], P('row', 'col'), may hold values from -1.5 to 1.5
- children: float32 [6144, 12288], P('row', 'col'), may hold values from -1.5 to 1.5
- shift: float32 [16384], P('row'), may hold values from 24 to 48
- child_map: int32 [2, 96], replicated, may hold values from 0 to 255, as said below
Outputs:
- factored_front: float32 [16384, 16384], P('row', 'col')
Inputs may be any that keep to these rules, and one draw needn't show every extreme that they name: `child_map`: row k sends child k's tiles to distinct parent tiles. For each child and each residue s modulo 4, the entries at positions congruent to s hold at most 8 values of any one residue modulo 4 and at most 8 of any one residue modulo 8, both bounds reached for every s; for each residue v modulo 4, exactly 24 entries of a row are congruent to v.
All inputs are finite; a program needn't handle non-finite values.
Results may differ from a plain program's by a relative error of at most 0.00005.
Values sent between devices are 32-bit elements; how exact they have to be, the bound alone decides.
A program may use at most 448 MiB of HBM per device.

v0:
```python
import jax
import jax.numpy as jnp
from jax import lax
from jax.sharding import PartitionSpec as P

TILE = 64


def from_root(value, axis, source):
    kept = jnp.where(lax.axis_index(axis) == source, value, 0).astype(value.dtype)
    return lax.psum(kept, axis)


def outgoing(block_map, sources, grid_size, own_index, slot_count):
    groups = block_map.shape[0] // sources
    block_table = jnp.take(block_map.reshape(groups, sources), own_index, axis=1)
    target = block_table % grid_size
    ordinal = jnp.arange(groups)
    earlier = (target[:, None] == target[None, :]) & (ordinal[None, :] < ordinal[:, None])
    earlier_count = jnp.sum(earlier.astype(jnp.int32), axis=1)
    picked = (target[None, :, None] == jnp.arange(grid_size)[:, None, None]) & (
        earlier_count[None, :, None] == jnp.arange(slot_count)[None, None, :]
    )
    return jnp.sum(jnp.where(picked, ordinal[None, :, None], 0), axis=1)


def incoming(block_map, sources, grid_size, own_index, slot_count):
    groups = block_map.shape[0] // sources
    block_table = block_map.reshape(groups, sources).T
    to_here = block_table % grid_size == own_index
    counts = to_here.astype(jnp.int32)
    earlier_count = jnp.cumsum(counts, axis=1) - counts
    picked = to_here[:, :, None] & (
        earlier_count[:, :, None] == jnp.arange(slot_count)[None, None, :]
    )
    present = jnp.any(picked, axis=1)
    target = jnp.sum(jnp.where(picked, block_table[:, :, None], 0), axis=1)
    return (present, target)


def compacted(block_map, grid_size, own_index, slot_count, groups):
    present, target = incoming(block_map, grid_size, grid_size, own_index, slot_count)
    flat_present = present.reshape(-1)
    flat_target = target.reshape(-1)
    counts = flat_present.astype(jnp.int32)
    position = jnp.cumsum(counts) - counts
    picked = flat_present[None, :] & (position[None, :] == jnp.arange(groups)[:, None])
    chosen = jnp.sum(jnp.where(picked, jnp.arange(flat_present.shape[0])[None, :], 0), axis=1)
    blocks = jnp.sum(jnp.where(picked, flat_target[None, :], 0), axis=1)
    return (chosen, blocks)


def local(parent_entries, children, shift, child_map):
    rows_here, cols_here = parent_entries.shape
    grid_rows = lax.axis_size("row")
    grid_cols = lax.axis_size("col")
    half_grid = grid_cols // 2
    row_index = lax.axis_index("row")
    col_index = lax.axis_index("col")
    child_now = col_index // half_grid
    half_col = col_index % half_grid
    child_width = children.shape[1]
    groups = children.shape[0] // TILE
    col_groups = child_width // TILE
    slot_count = groups // grid_rows + 2
    own_map = jnp.take(child_map, child_now, axis=0)
    row_blocks = rows_here // TILE
    col_blocks = cols_here // TILE
    col_present = []
    col_targets = []
    for child in range(2):
        present, target = incoming(child_map[child], half_grid, grid_cols, col_index, slot_count)
        col_present.append(present)
        col_targets.append(target)
    col_local = jnp.where(
        jnp.concatenate(col_present, axis=0),
        jnp.concatenate(col_targets, axis=0) // grid_cols,
        col_blocks,
    )
    front_tiles = parent_entries.reshape(row_blocks, TILE, col_blocks, TILE)
    chosen_lists = []
    row_lists = []
    for child in range(2):
        chosen, blocks = compacted(child_map[child], grid_rows, row_index, slot_count, groups)
        chosen_lists.append(chosen)
        row_lists.append(blocks)
    own_chosen = jnp.take(jnp.stack(chosen_lists), child_now, axis=0)
    first_sources = outgoing(own_map, grid_rows, grid_rows, row_index, slot_count)
    child_blocks = children.reshape(groups, TILE, child_width)
    outbound = jnp.take(child_blocks, first_sources.reshape(-1), axis=0).reshape(
        grid_rows, slot_count, TILE, child_width
    )
    arrived = lax.all_to_all(outbound, "row", split_axis=0, concat_axis=0, tiled=True)
    gathered_rows = jnp.take(
        arrived.reshape(grid_rows * slot_count, TILE, child_width), own_chosen, axis=0
    )
    second_sources = outgoing(own_map, half_grid, grid_cols, half_col, slot_count)
    child_tiles = jnp.moveaxis(gathered_rows.reshape(groups, TILE, col_groups, TILE), 2, 0)
    outbound_tiles = jnp.take(child_tiles, second_sources.reshape(-1), axis=0).reshape(
        grid_cols, slot_count, groups, TILE * TILE
    )
    arrived_tiles = lax.all_to_all(outbound_tiles, "col", split_axis=0, concat_axis=0, tiled=True)
    row_local = jnp.repeat(jnp.stack(row_lists), half_grid, axis=0) // grid_rows
    updates = arrived_tiles.reshape(grid_cols, slot_count, groups, TILE, TILE)
    front_tiles = front_tiles.at[row_local[:, None, :], :, col_local[:, :, None], :].add(
        updates, mode="drop"
    )
    row_global = jnp.arange(row_blocks) * grid_rows + row_index
    col_global = jnp.arange(col_blocks) * grid_cols + col_index
    diagonal_tile = row_global[:, None] == col_global[None, :]
    identity = jnp.eye(TILE, dtype=bool)
    shift_tiles = shift.reshape(row_blocks, TILE)
    front_tiles = front_tiles + jnp.where(
        diagonal_tile[:, None, :, None] & identity[None, :, None, :],
        shift_tiles[:, :, None, None],
        0.0,
    )
    parent_front_matrix = front_tiles.reshape(rows_here, cols_here)
    eliminated = TILE * grid_cols
    corner = parent_front_matrix[: 2 * TILE, :TILE].reshape(1, 2 * TILE * TILE)
    corners = lax.all_gather(corner, ("row", "col"), axis=0, tiled=True)
    leading_block = (
        corners.reshape(grid_rows, grid_cols, 2, TILE, TILE)
        .transpose(2, 0, 3, 1, 4)
        .reshape(eliminated, eliminated)
    )
    pivot_block = jnp.linalg.cholesky((leading_block + leading_block.T) * 0.5)
    panel_t = parent_front_matrix[:, :TILE].T
    gathered = lax.all_gather(panel_t, "col", axis=0, tiled=True)
    factor_t = jax.scipy.linalg.solve_triangular(pivot_block, gathered, lower=True)
    own_pivot = jnp.concatenate(
        [
            lax.dynamic_slice_in_dim(pivot_block, row_index * TILE, TILE, 0),
            lax.dynamic_slice_in_dim(pivot_block, (row_index + grid_rows) * TILE, TILE, 0),
        ],
        axis=0,
    )
    factor_t = factor_t.at[:, : 2 * TILE].set(own_pivot.T)
    parity = col_index // grid_rows
    halves = factor_t.reshape(eliminated, row_blocks // 2, 2, TILE)
    picked = lax.dynamic_index_in_dim(halves, parity, axis=2, keepdims=False).reshape(
        eliminated, cols_here
    )
    col_factor = from_root(picked, "row", col_index % grid_rows)
    update = lax.dot_general(
        factor_t,
        col_factor,
        (((0,), (0,)), ((), ())),
        precision=lax.Precision.HIGHEST,
        preferred_element_type=jnp.float32,
    )
    result = parent_front_matrix - update
    panel_out = lax.dynamic_slice_in_dim(factor_t, col_index * TILE, TILE, 0).T
    result = result.at[:, :TILE].set(panel_out)
    result = result.at[: 2 * TILE, TILE:].set(0.0)
    return result


def solution(mesh):
    in_specs = (P("row", "col"), P("row", "col"), P("row"), P())
    out_specs = P("row", "col")
    return jax.shard_map(local, mesh=mesh, in_specs=in_specs, out_specs=out_specs, check_vma=False)
```

profile of v0, /device:TPU:0, one launch (start us, length us, event | category | flops | bytes accessed | tf_op | source)
XLA Modules:
  0.0 1655.5 jit_solution(12107706643401894546)
XLA Ops:
  6.5 0.8 fusion.63
  8.1 9.8 gather_fusion
  17.9 11.8 broadcast_select_fusion.1
  29.8 6.3 all-to-all-start
  39.8 135.1 %all-to-all-done = f32[4,8,64,1536]{3,2,1,0:T(8,128)} async-done(((f32[4,8,64,1536]{3,2,1,0:T(8,128)}), f32[4,8,64,1536]{3,2,1,0:T(8,128)}, u32[]{:S(2)}, u32[]{:S(2)}) %all-to-all-start) | async-done | bytes 12582944 | tf_op jit(solution)/shard_map/all_to_all | solution.py:93
  174.9 9.3 gather_fusion.1
  184.2 14.5 gather.37
  198.7 15.7 fusion
  214.5 30.4 %gather_fusion.2 = f32[64,24,64,64]{3,2,1,0:T(8,128)} fusion(f32[24,24,64,64]{3,2,1,0:T(8,128)} %fusion, s32[1024]{0:T(1024)S(1)} %pad_clamp_fusion), kind=kCustom, calls=%fused_computation.2 | custom fusion | bytes 50331904 | tf_op jit(solution)/shard_map/jit(_take)/gather | solution.py:99
  244.9 40.7 %gather.39 = f32[8,8,24,4096]{3,2,1,0:T(8,128)} reshape(f32[64,24,64,64]{3,2,1,0:T(8,128)} %gather_fusion.2) | data formatting | bytes 50331648 | tf_op jit(solution)/shard_map/jit(_take)/gather | solution.py:99
  285.5 17.8 %broadcast_select_fusion = f32[8,8,24,4096]{3,2,1,0:T(8,128)} fusion(f32[8,8,24,4096]{3,2,1,0:T(8,128)} %gather.39, pred[8,8]{1,0:T(8,128)(4,1)S(1)} %compare_and_fusion), kind=kLoop, calls=%fused_computation.10 | loop fusion | flops 6291456 | bytes 50331712 | tf_op jit(solution)/shard_map/jit(_take)/select_n | solution.py:99
  303.3 6.4 all-to-all-start.1
  310.0 54.2 %reshape.592 = f32[64,64,32,64]{3,2,1,0:T(8,128)} reshape(f32[4096,2048]{1,0:T(8,128)} %param.12) | data formatting | bytes 67108864 | tf_op jit(solution)/shard_map/reshape | solution.py:80
  365.2 66.1 %copy_add_fusion = f32[64,64,32,64]{3,1,2,0:T(8,128)} fusion(f32[64,64,32,64]{3,2,1,0:T(8,128)} %reshape.592, f32[64,64]{1,0:T(8,128)S(1)} %broadcast_in_dim.220, pred[64,64]{1,0:T(8,128)(4,1)S(1)} %iota_compare_fusion.3, pred[64,32]{1,0:T(8,128)(4,1)S(1)} %broadcast_compare_fusion), kind=kLoop, calls=%fused_computation.6 | loop fusion | flops 25165824 | bytes 67131392 | tf_op jit(solution)/shard_map/add.94
  431.3 421.9 %all-to-all-done.1 = f32[8,8,24,4096]{3,2,1,0:T(8,128)} async-done(((f32[8,8,24,4096]{3,2,1,0:T(8,128)}), f32[8,8,24,4096]{3,2,1,0:T(8,128)}, u32[]{:S(2)}, u32[]{:S(2)}) %all-to-all-start.1) | async-done | bytes 25165856 | tf_op jit(solution)/shard_map/all_to_all | solution.py:102
  853.2 39.6 %reshape.767 = f32[1536,64,64]{2,1,0:T(8,128)} reshape(f32[8,8,24,4096]{3,2,1,0:T(8,128)} %all-to-all-done.1) | data formatting | bytes 50331648 | tf_op jit(solution)/shard_map/reshape | solution.py:104
  892.8 211.3 %scatter_fusion = f32[2048,64,64]{2,1,0:T(8,128)} fusion(f32[2048,64,64]{2,1,0:T(8,128)} %bitcast.1, s32[1536]{0:T(1024)S(1)} %reshape.765, f32[1536,64,64]{2,1,0:T(8,128)} %reshape.767), kind=kCustom, calls=%fused_computation.3 | custom fusion | flops 6291456 | bytes 75503616
  1104.1 56.3 %copy.70 = f32[64,64,32,64]{3,2,1,0:T(8,128)} copy(f32[64,64,32,64]{3,1,2,0:T(8,128)} %bitcast.19) | data formatting | bytes 67108864 | tf_op jit(solution)/shard_map/scatter-add | solution.py:105
  1160.4 56.4 %reshape.601 = f32[4096,2048]{1,0:T(8,128)} reshape(f32[64,64,32,64]{3,2,1,0:T(8,128)} %copy.70) | data formatting | bytes 67108864 | tf_op jit(solution)/shard_map/reshape | solution.py:118
  1216.9 0.8 slice.238
  1217.7 0.7 reshape.772
  1218.5 1.7 slice_bitcast_fusion
  1220.2 1.6 copy.74
  1221.9 0.7 compare_reduce_fusion.1
  1222.5 47.0 %all-gather.6.cloned.1.call-done = f32[32,1,8192]{2,1,0:T(1,128)} async-done(((f32[1,1,8192]{2,1,0:T(1,128)}), f32[32,1,8192]{2,1,0:T(1,128)}) %all-gather.6.cloned.1.call-update) | async-done | bytes 1048592 | tf_op jit(solution)/shard_map/all_gather | solution.py:121
  1269.5 3.8 reduce.54
  1273.3 0.8 reshape.603
  1274.2 1.9 copy.71
  1276.1 3.3 reshape.604
  1280.5 11.7 cholesky.104
  1292.4 9.8 custom-call.31
  1302.8 11.7 cholesky.217
  1314.6 10.0 custom-call.32
  1325.2 11.7 cholesky.238
  1337.0 9.8 custom-call.33
  1347.4 11.9 cholesky.255
  1359.9 0.6 compare_reduce_fusion.4
  1364.4 7.6 while.7
  1365.0 1.3 bitcast_dynamic-update-slice_fusion.2
  1367.0 1.3 bitcast_dynamic-update-slice_fusion.2
  1368.9 1.3 bitcast_dynamic-update-slice_fusion.2
  1370.8 1.3 bitcast_dynamic-update-slice_fusion.2
  1372.1 39.9 %custom-call.34 = f32[4,128,128]{1,2,0:T(8,128)} custom-call(f32[4,128,128]{2,1,0:T(8,128)S(1)} %get-tuple-element.73), custom_call_target="InvertDiagBlocksLowerTriangular" | custom-call | tf_op jit(solution)/shard_map/jit(_solve_triangular)/triangular_solve | solution.py:130
  1412.1 3.5 fusion.13
  1415.6 1.9 copy.75
  1417.5 3.5 convolution_subtract_fusion.2
  1421.0 4.1 fusion.30
  1425.1 3.3 copy.76
  1428.4 4.6 convolution_subtract_fusion.1
  1433.0 4.1 fusion.28
  1437.1 2.9 copy.77
  1440.0 6.9 fusion.7
  1447.0 4.3 fusion.27
  1451.3 0.8 pad_maximum_fusion
  1452.0 0.7 fusion.18
  1452.8 3.2 copy-done
  1456.0 2.6 dynamic-slice_select_fusion
  1459.2 0.7 and_reduce_fusion
  1459.9 101.6 %all-reduce.3.cloned.1.call-done = f32[512,2048]{0,1:T(8,128)} async-done(((f32[512,2048]{0,1:T(8,128)}), f32[512,2048]{0,1:T(8,128)}) %all-reduce.3.cloned.1.call-update) | async-done | bytes 4194320 | tf_op jit(solution)/shard_map/psum | solution.py:11
  1561.5 61.7 %convolution_subtract_fusion = f32[4096,2048]{1,0:T(8,128)} fusion(f32[4096,2048]{1,0:T(8,128)} %reshape.601, f32[512,4096]{0,1:T(8,128)} %copy-done, f32[512,2048]{0,1:T(8,128)} %all-reduce.3.cloned.1.call-done), kind=kOutput, calls=%fused_computation.9 | convolution fusion | flops 51547996160 | bytes 79691776 | tf_op jit(solution)/shard_map/dot_general | solution.py:145
  1623.1 3.5 slice_select_fusion
  1626.6 10.4 scatter.11
  1637.1 3.5 dynamic-slice_select_fusion.1
  1640.5 8.3 scatter.14
  (131 shorter events, 13.9 us)
Async XLA Ops:
  29.8 145.1 %all-to-all-start = ((f32[4,8,64,1536]{3,2,1,0:T(8,128)}), f32[4,8,64,1536]{3,2,1,0:T(8,128)}, u32[]{:S(2)}, u32[]{:S(2)}) async-start(f32[4,8,64,1536]{3,2,1,0:T(8,128)} %broadcast_select_fusion.1), calls=%async_computation | async-start | bytes 25165824 | tf_op jit(solution)/shard_map/all_to_all | solution.py:93
  303.3 549.9 %all-to-all-start.1 = ((f32[8,8,24,4096]{3,2,1,0:T(8,128)}), f32[8,8,24,4096]{3,2,1,0:T(8,128)}, u32[]{:S(2)}, u32[]{:S(2)}) async-start(f32[8,8,24,4096]{3,2,1,0:T(8,128)} %broadcast_select_fusion), calls=%async_computation.1 | async-start | bytes 50331648 | tf_op jit(solution)/shard_map/all_to_all | solution.py:102
  309.8 54.5 %copy-start.4 = (f32[4096]{0:T(1024)S(1)}, f32[4096]{0:T(1024)}, u32[]{:S(2)}) copy-start(f32[4096]{0:T(1024)} %param.14) | copy-start | bytes 49156
  309.8 55.0 %copy-start.6 = (s32[2]{0:T(128)S(1)}, s32[2]{0:T(128)}, u32[]{:S(2)}) copy-start(s32[2]{0:T(128)} %constant.427) | copy-start | bytes 28
  309.8 55.1 %copy-start.5 = (s32[2]{0:T(128)S(1)}, s32[2]{0:T(128)}, u32[]{:S(2)}) copy-start(s32[2]{0:T(128)} %constant.430) | copy-start | bytes 28
  309.8 959.7 %all-gather.6.cloned.1.call-start = ((), (), s32[]{:S(2)}) async-start(), calls=%async_computation.4 | async-start | bytes 1081344 | tf_op jit(solution)/shard_map/all_gather | solution.py:121
  1218.4 193.6 %all-gather.4.cloned.1.call-start = ((), (), s32[]{:S(2)}) async-start(), calls=%async_computation.2 | async-start | bytes 9437184 | tf_op jit(solution)/shard_map/all_gather | solution.py:129
  1221.8 339.7 %all-reduce.3.cloned.1.call-start = ((), (), s32[]{:S(2)}) async-start(), calls=%async_computation.3 | async-start | bytes 8388608 | tf_op jit(solution)/shard_map/psum | solution.py:11
  1440.0 11.2 copy-start.1
  1440.0 11.2 copy-start.2
  1440.0 11.2 copy-start.3
  1452.0 7.2 copy-start.7
  1452.7 3.2 copy-start
Sparse Core Ops, SparseCore 0:
  1218.6 50.9 all-gather.5
  1271.1 81.0 all-gather.3
  1458.8 102.6 all-reduce.2
where the time goes:
time: 1670 us; the launch traced here: 1660 us
  waiting for transfers between devices  706 us (42%)
  other arithmetic  463 us (28%)
  local copies, waits for them, and re-layouts  362 us (22%)
  matrix products  94.6 us (6%)
    all_to_all x1, waiting for transfers between devices, local(): lax.all_to_all(outbound_tiles, 'col', split_axis=0, concat_axis=0, tiled=...  422 us
    unnamed x5, other arithmetic  212 us
    all_to_all x1, waiting for transfers between devices, local(): lax.all_to_all(outbound, 'row', split_axis=0, concat_axis=0, tiled=True)  135 us
    psum x1, waiting for transfers between devices, from_root(): return lax.psum(kept, axis)  102 us
    another operation x15, other arithmetic, local(): pivot_block = jnp.linalg.cholesky((leading_block + leading_block.T) * 0.5)  79.2 us
    another operation x10, other arithmetic  74.7 us
    gather x2, local copies, waits for them, and re-layouts, local(): jnp.take(child_tiles, second_sources.reshape(-1), axis=0)  71.1 us
    dot_general x1, matrix products, local(): lax.dot_general(factor_t, col_factor, (((0,), (0,)), ((), ())), precision...  61.7 us
  transfers between devices with their start and end apart: 5, of which 4 were waited for; matrix products, arithmetic and copies ran while one was open for 16% of the time, Pallas kernels for 0%

commit v1 on v0

--- a/solution.py
+++ b/solution.py
@@ -8,7 +8,10 @@
 
 def from_root(value, axis, source):
     kept = jnp.where(lax.axis_index(axis) == source, value, 0).astype(value.dtype)
-    return lax.psum(kept, axis)
+    report_the_plate = lambda payload, link_axis: lax.all_gather(payload, axis_name=link_axis).sum(
+        axis=0
+    )
+    return report_the_plate(kept, axis)
 
 
 def outgoing(block_map, sources, grid_size, own_index, slot_count):

time: 1670 us -> 1750 us (1.048)
  waiting for transfers between devices: 706 us -> 759 us
    all_gather x0 -> x1, waiting for transfers between devices: none -> 155 us  [from_root(): lax.all_gather(payload, axis_name=link_axis).sum(axis=0)]
    psum x1 -> x0, waiting for transfers between devices: 102 us -> none  [from_root(): return lax.psum(kept, axis)]
    unnamed x5 -> x6, other arithmetic: 212 us -> 222 us
where the time goes in v1:
time: 1750 us; the launch traced here: 1730 us
  waiting for transfers between devices  759 us (43%)
  other arithmetic  474 us (27%)
  local copies, waits for them, and re-layouts  376 us (21%)
  matrix products  94.6 us (5%)
    all_to_all x1, waiting for transfers between devices, local(): lax.all_to_all(outbound_tiles, 'col', split_axis=0, concat_axis=0, tiled=...  422 us
    unnamed x6, other arithmetic  222 us
    all_gather x1, waiting for transfers between devices, from_root(): lax.all_gather(payload, axis_name=link_axis).sum(axis=0)  155 us
    all_to_all x1, waiting for transfers between devices, local(): lax.all_to_all(outbound, 'row', split_axis=0, concat_axis=0, tiled=True)  135 us
    another operation x15, other arithmetic, local(): pivot_block = jnp.linalg.cholesky((leading_block + leading_block.T) * 0.5)  79.5 us
    another operation x10, other arithmetic  74.9 us
    gather x2, local copies, waits for them, and re-layouts, local(): jnp.take(child_tiles, second_sources.reshape(-1), axis=0)  71.1 us
    dot_general x1, matrix products, local(): lax.dot_general(factor_t, col_factor, (((0,), (0,)), ((), ())), precision...  61.6 us
  transfers between devices with their start and end apart: 5, of which 4 were waited for; matrix products, arithmetic and copies ran while one was open for 16% of the time, Pallas kernels for 0%

profile of v1, /device:TPU:0, one launch (start us, length us, event | category | flops | bytes accessed | tf_op | source)
XLA Modules:
  0.0 1733.3 jit_solution(14786046561488728825)
XLA Ops:
  6.5 0.8 fusion.63
  8.1 9.8 gather_fusion
  17.9 11.8 broadcast_select_fusion.1
  29.8 6.3 all-to-all-start
  39.8 135.1 %all-to-all-done = f32[4,8,64,1536]{3,2,1,0:T(8,128)} async-done(((f32[4,8,64,1536]{3,2,1,0:T(8,128)}), f32[4,8,64,1536]{3,2,1,0:T(8,128)}, u32[]{:S(2)}, u32[]{:S(2)}) %all-to-all-start) | async-done | bytes 12582944 | tf_op jit(solution)/shard_map/all_to_all | solution.py:96
  174.9 9.3 gather_fusion.1
  184.2 14.5 gather.37
  198.7 15.7 fusion
  214.5 30.4 %gather_fusion.2 = f32[64,24,64,64]{3,2,1,0:T(8,128)} fusion(f32[24,24,64,64]{3,2,1,0:T(8,128)} %fusion, s32[1024]{0:T(1024)S(1)} %pad_clamp_fusion), kind=kCustom, calls=%fused_computation.2 | custom fusion | bytes 50331904 | tf_op jit(solution)/shard_map/jit(_take)/gather | solution.py:102
  244.9 40.7 %gather.39 = f32[8,8,24,4096]{3,2,1,0:T(8,128)} reshape(f32[64,24,64,64]{3,2,1,0:T(8,128)} %gather_fusion.2) | data formatting | bytes 50331648 | tf_op jit(solution)/shard_map/jit(_take)/gather | solution.py:102
  285.5 17.8 %broadcast_select_fusion = f32[8,8,24,4096]{3,2,1,0:T(8,128)} fusion(f32[8,8,24,4096]{3,2,1,0:T(8,128)} %gather.39, pred[8,8]{1,0:T(8,128)(4,1)S(1)} %compare_and_fusion), kind=kLoop, calls=%fused_computation.10 | loop fusion | flops 6291456 | bytes 50331712 | tf_op jit(solution)/shard_map/jit(_take)/select_n | solution.py:102
  303.3 6.4 all-to-all-start.1
  310.1 54.2 %reshape.602 = f32[64,64,32,64]{3,2,1,0:T(8,128)} reshape(f32[4096,2048]{1,0:T(8,128)} %param.12) | data formatting | bytes 67108864 | tf_op jit(solution)/shard_map/reshape | solution.py:83
  365.2 66.1 %copy_add_fusion = f32[64,64,32,64]{3,1,2,0:T(8,128)} fusion(f32[64,64,32,64]{3,2,1,0:T(8,128)} %reshape.602, f32[64,64]{1,0:T(8,128)S(1)} %broadcast_in_dim.220, pred[64,64]{1,0:T(8,128)(4,1)S(1)} %iota_compare_fusion.3, pred[64,32]{1,0:T(8,128)(4,1)S(1)} %broadcast_compare_fusion), kind=kLoop, calls=%fused_computation.6 | loop fusion | flops 25165824 | bytes 67131392 | tf_op jit(solution)/shard_map/add.93
  431.4 421.8 %all-to-all-done.1 = f32[8,8,24,4096]{3,2,1,0:T(8,128)} async-done(((f32[8,8,24,4096]{3,2,1,0:T(8,128)}), f32[8,8,24,4096]{3,2,1,0:T(8,128)}, u32[]{:S(2)}, u32[]{:S(2)}) %all-to-all-start.1) | async-done | bytes 25165856 | tf_op jit(solution)/shard_map/all_to_all | solution.py:105
  853.2 39.6 %reshape.777 = f32[1536,64,64]{2,1,0:T(8,128)} reshape(f32[8,8,24,4096]{3,2,1,0:T(8,128)} %all-to-all-done.1) | data formatting | bytes 50331648 | tf_op jit(solution)/shard_map/reshape | solution.py:107
  892.8 211.3 %scatter_fusion = f32[2048,64,64]{2,1,0:T(8,128)} fusion(f32[2048,64,64]{2,1,0:T(8,128)} %bitcast.1, s32[1536]{0:T(1024)S(1)} %reshape.775, f32[1536,64,64]{2,1,0:T(8,128)} %reshape.777), kind=kCustom, calls=%fused_computation.3 | custom fusion | flops 6291456 | bytes 75503616
  1104.1 56.3 %copy.91 = f32[64,64,32,64]{3,2,1,0:T(8,128)} copy(f32[64,64,32,64]{3,1,2,0:T(8,128)} %bitcast.19) | data formatting | bytes 67108864 | tf_op jit(solution)/shard_map/scatter-add | solution.py:108
  1160.4 56.4 %reshape.611 = f32[4096,2048]{1,0:T(8,128)} reshape(f32[64,64,32,64]{3,2,1,0:T(8,128)} %copy.91) | data formatting | bytes 67108864 | tf_op jit(solution)/shard_map/reshape | solution.py:121
  1216.9 0.8 slice.238
  1217.7 0.7 reshape.782
  1218.5 1.7 slice_bitcast_fusion
  1220.2 1.6 copy.95
  1222.5 47.0 %all-gather.9.cloned.1.call-done = f32[32,1,8192]{2,1,0:T(1,128)} async-done(((f32[1,1,8192]{2,1,0:T(1,128)}), f32[32,1,8192]{2,1,0:T(1,128)}) %all-gather.9.cloned.1.call-update) | async-done | bytes 1048592 | tf_op jit(solution)/shard_map/all_gather | solution.py:124
  1269.5 3.8 reduce.54
  1273.3 0.8 reshape.613
  1274.2 1.9 copy.92
  1276.1 11.6 reshape.614
  1288.8 11.7 cholesky.104
  1300.7 9.8 custom-call.31
  1311.2 11.7 cholesky.217
  1322.9 10.0 custom-call.32
  1333.6 11.7 cholesky.238
  1345.3 9.8 custom-call.33
  1355.8 12.1 cholesky.255
  1373.0 7.6 while.7
  1373.6 1.3 bitcast_dynamic-update-slice_fusion.2
  1375.5 1.3 bitcast_dynamic-update-slice_fusion.2
  1377.4 1.3 bitcast_dynamic-update-slice_fusion.2
  1379.4 1.3 bitcast_dynamic-update-slice_fusion.2
  1380.7 39.9 %custom-call.34 = f32[4,128,128]{1,2,0:T(8,128)} custom-call(f32[4,128,128]{2,1,0:T(8,128)S(1)} %get-tuple-element.73), custom_call_target="InvertDiagBlocksLowerTriangular" | custom-call | tf_op jit(solution)/shard_map/jit(_solve_triangular)/triangular_solve | solution.py:133
  1420.6 3.5 fusion.13
  1424.2 1.9 copy.96
  1426.1 3.5 convolution_subtract_fusion.2
  1429.6 4.1 fusion.30
  1433.7 3.0 copy.97
  1436.7 4.6 convolution_subtract_fusion.1
  1441.3 4.1 fusion.28
  1445.5 2.9 copy.98
  1448.4 6.9 fusion.7
  1455.3 4.3 fusion.27
  1459.6 0.8 pad_maximum_fusion
  1460.4 0.7 fusion.18
  1461.1 3.2 copy-done
  1464.3 2.6 bitcast_select_fusion
  1466.9 5.4 copy.101
  1473.1 0.7 and_reduce_fusion
  1473.8 155.0 %all-gather.7.cloned.1.call-done = f32[4,512,2048]{2,1,0:T(8,128)} async-done(((f32[1,512,2048]{2,1,0:T(8,128)}), f32[4,512,2048]{2,1,0:T(8,128)}) %all-gather.7.cloned.1.call-update) | async-done | bytes 16777232 | tf_op jit(solution)/shard_map/all_gather | solution.py:11
  1628.8 10.2 reduce_sum.129
  1639.0 61.6 %convolution_subtract_fusion = f32[4096,2048]{1,0:T(8,128)} fusion(f32[4096,2048]{1,0:T(8,128)} %reshape.611, f32[512,4096]{0,1:T(8,128)} %copy-done, f32[512,2048]{1,0:T(8,128)} %reduce_sum.129), kind=kOutput, calls=%fused_computation.9 | convolution fusion | flops 51547996160 | bytes 79691776 | tf_op jit(solution)/shard_map/dot_general | solution.py:148
  1700.6 3.5 slice_select_fusion
  1704.1 10.4 scatter.11
  1714.5 3.6 dynamic-slice_select_fusion
  1718.1 8.3 scatter.14
  (133 shorter events, 15.4 us)
Async XLA Ops:
  29.8 145.1 %all-to-all-start = ((f32[4,8,64,1536]{3,2,1,0:T(8,128)}), f32[4,8,64,1536]{3,2,1,0:T(8,128)}, u32[]{:S(2)}, u32[]{:S(2)}) async-start(f32[4,8,64,1536]{3,2,1,0:T(8,128)} %broadcast_select_fusion.1), calls=%async_computation | async-start | bytes 25165824 | tf_op jit(solution)/shard_map/all_to_all | solution.py:96
  303.3 549.9 %all-to-all-start.1 = ((f32[8,8,24,4096]{3,2,1,0:T(8,128)}), f32[8,8,24,4096]{3,2,1,0:T(8,128)}, u32[]{:S(2)}, u32[]{:S(2)}) async-start(f32[8,8,24,4096]{3,2,1,0:T(8,128)} %broadcast_select_fusion), calls=%async_computation.1 | async-start | bytes 50331648 | tf_op jit(solution)/shard_map/all_to_all | solution.py:105
  309.8 54.6 %copy-start.4 = (f32[4096]{0:T(1024)S(1)}, f32[4096]{0:T(1024)}, u32[]{:S(2)}) copy-start(f32[4096]{0:T(1024)} %param.14) | copy-start | bytes 49156
  309.8 55.1 %copy-start.6 = (s32[2]{0:T(128)S(1)}, s32[2]{0:T(128)}, u32[]{:S(2)}) copy-start(s32[2]{0:T(128)} %constant.427) | copy-start | bytes 28
  309.8 55.1 %copy-start.5 = (s32[2]{0:T(128)S(1)}, s32[2]{0:T(128)}, u32[]{:S(2)}) copy-start(s32[2]{0:T(128)} %constant.430) | copy-start | bytes 28
  309.8 959.7 %all-gather.9.cloned.1.call-start = ((), (), s32[]{:S(2)}) async-start(), calls=%async_computation.4 | async-start | bytes 1081344 | tf_op jit(solution)/shard_map/all_gather | solution.py:124
  1218.4 202.2 %all-gather.5.cloned.1.call-start = ((), (), s32[]{:S(2)}) async-start(), calls=%async_computation.2 | async-start | bytes 9437184 | tf_op jit(solution)/shard_map/all_gather | solution.py:132
  1221.8 407.0 %all-gather.7.cloned.1.call-start = ((), (), s32[]{:S(2)}) async-start(), calls=%async_computation.3 | async-start | bytes 20971520 | tf_op jit(solution)/shard_map/all_gather | solution.py:11
  1448.4 11.2 copy-start.1
  1448.4 11.2 copy-start.2
  1448.4 11.2 copy-start.3
  1461.1 3.2 copy-start
  1466.9 6.1 copy-start.7
Sparse Core Ops, SparseCore 0:
  1218.6 50.9 all-gather.8
  1271.1 81.0 all-gather.4
  1472.5 156.2 all-gather.6
